TPU v7x, 32 devices: a whole 2x2x4 slice. The times are simulated.
32 devices in a mesh: group: 2 (over x), patch: 16 (over z, y, core).
Axes of the slice: x: 2, y: 2, z: 4, core: 2. Of those that a mesh axis runs over, the one named last changes fastest.
Arguments:
- queries: bfloat16 [1024, 1536], P(('group', 'patch')), parts along dimension 0, may hold values from -6 to 6
- keys: bfloat16 [1024, 1536], P(('group', 'patch')), parts along dimension 0, may hold values from -6 to 6
- values: bfloat16 [1024, 1536], P(('group', 'patch')), parts along dimension 0, may hold values from -6 to 6
- stale_keys: bfloat16 [1024, 1536], P(('group', 'patch')), parts along dimension 0, may hold values from -6 to 6
- stale_values: bfloat16 [1024, 1536], P(('group', 'patch')), parts along dimension 0, may hold values from -6 to 6
- text_keys: bfloat16 [32, 512, 1536], P(('group', 'patch')), parts along dimension 0, may hold values from -200 to 200
- text_values: bfloat16 [32, 512, 1536], P(('group', 'patch')), parts along dimension 0, may hold values from -6 to 6
- prompt_device: int32 [2], P('group'), parts along dimension 0, may hold values from 0 to 15
- patch_owner: int32 [32], P('group'), parts along dimension 0, may hold values from 0 to 15, each once
- step: int32 [2], P('group'), parts along dimension 0, may hold values from 0 to 27
- q_gain: float32 [128], replicated, may hold values from 1 to 2.5
- k_gain: float32 [128], replicated, may hold values from 1 to 2.5
- gate_table: float32 [28, 1536], replicated, may hold values from 0.5 to 2
Outputs:
- attended: bfloat16 [1024, 1536], P(('group', 'patch')), parts along dimension 0
There are 2 independent parts, one for each index of `group`. A program takes and returns all parts, laid end to end along the dimension named above; an argument that names none is the same for every part. Nothing has to cross between parts.
Inputs may be any that keep to these rules, and one draw needn't show every extreme that they name: `patch_owner`: A permutation: each patch is held by exactly one device.
All inputs are finite; a program needn't handle non-finite values.
Results may differ from a plain program's by a relative error of at most 0.009.
Values may be sent and summed in bfloat16 or wider, within the bound.
No kernel may reach another device: no remote copies, remote signals or barrier semaphores. Data moves between devices by JAX's collectives and lax.ppermute only.
A program may use at most 128 MiB of HBM per device.

v0:
```python
import jax
import jax.numpy as jnp
from jax import lax
from jax.sharding import PartitionSpec as P

DH = 128
GRID_W = 64
epsilon = 1e-06


def from_partner(shard, axis, bit):
    return lax.ppermute(shard, axis, [(i, i ^ 1 << bit) for i in range(lax.axis_size(axis))])


def broadcast(shard, axis, root):
    mine = lax.axis_index(axis) == root
    return lax.psum(jnp.where(mine, shard, jnp.zeros_like(shard)), axis)


def rms_norm(values_in, gain):
    row_count = values_in.shape[0]
    heads_in = values_in.astype(jnp.float32).reshape(row_count, -1, DH)
    mean_square = jnp.mean(heads_in * heads_in, axis=-1, keepdims=True)
    return heads_in * lax.rsqrt(mean_square + epsilon) * gain


def rope_tables(grid_index):
    grid_row = (grid_index // GRID_W).astype(jnp.float32)
    grid_col = (grid_index % GRID_W).astype(jnp.float32)
    omega = 10000.0 ** (-2.0 * jnp.arange(28, dtype=jnp.float32) / 56.0)
    angle = jnp.concatenate(
        [
            jnp.zeros((grid_index.shape[0], 8), jnp.float32),
            grid_row[:, None] * omega,
            grid_col[:, None] * omega,
        ],
        axis=1,
    )
    return (jnp.cos(angle), jnp.sin(angle))


def rotate(normed, cosine, sine_part):
    row_count, head_count = (normed.shape[0], normed.shape[1])
    paired = normed.reshape(row_count, head_count, DH // 2, 2)
    real_part = paired[..., 0]
    imag_part = paired[..., 1]
    cos_heads = cosine[:, None, :]
    sin_heads = sine_part[:, None, :]
    rotated = jnp.stack(
        [
            cos_heads * real_part - sin_heads * imag_part,
            sin_heads * real_part + cos_heads * imag_part,
        ],
        axis=-1,
    )
    return rotated.reshape(row_count, head_count * DH).astype(jnp.bfloat16)


def partial_softmax(query_local, key_rows, value_rows, key_valid):
    key_count = key_rows.shape[0]
    head_count = query_local.shape[1]
    key_heads = key_rows.reshape(key_count, head_count, DH)
    value_heads = value_rows.reshape(key_count, head_count, DH)
    scores = jnp.einsum(
        "qhd,khd->hqk", query_local, key_heads, preferred_element_type=jnp.float32
    ) * DH ** (-0.5)
    scores = jnp.where(key_valid[None], scores, -1e30)
    highest = jnp.max(scores, axis=-1)
    weights = jnp.where(key_valid[None], jnp.exp(scores - highest[..., None]), 0.0)
    totals = jnp.sum(weights, axis=-1)
    summed = jnp.einsum(
        "hqk,khd->hqd",
        weights.astype(jnp.bfloat16),
        value_heads,
        preferred_element_type=jnp.float32,
    )
    return (highest, totals, summed)


def combine_parts(earlier, later):
    highest = jnp.maximum(earlier[0], later[0])
    factor_early = jnp.exp(earlier[0] - highest)
    factor_late = jnp.exp(later[0] - highest)
    totals = earlier[1] * factor_early + later[1] * factor_late
    summed = earlier[2] * factor_early[..., None] + later[2] * factor_late[..., None]
    return (highest, totals, summed)


def split_swap(piece, bit):
    return from_partner(piece, "patch", bit)


def join_swap(piece, bit):
    return from_partner(piece, "patch", bit)


def order_pair(own_bit, mine, other, axis):
    return jnp.where(own_bit == 0, jnp.stack([mine, other], axis), jnp.stack([other, mine], axis))


def split_heads(stacked, device_index):
    count, tok_rows, feat = stacked.shape
    quarter_width = feat // 4
    low_bit = device_index % 2
    high_bit = device_index // 2 % 2
    shaped = stacked.reshape(count, tok_rows, 2, 2, quarter_width)
    kept = lax.dynamic_index_in_dim(shaped, low_bit, 3, keepdims=False)
    sent = lax.dynamic_index_in_dim(shaped, 1 - low_bit, 3, keepdims=False)
    first = order_pair(low_bit, kept, split_swap(sent, 0), 1)
    kept = lax.dynamic_index_in_dim(first, high_bit, 3, keepdims=False)
    sent = lax.dynamic_index_in_dim(first, 1 - high_bit, 3, keepdims=False)
    second = order_pair(high_bit, kept, split_swap(sent, 1), 1)
    return second.reshape(count, 4 * tok_rows, quarter_width)


def join_heads(block, device_index):
    quad_rows, quarter_width = block.shape
    tok_rows = quad_rows // 4
    low_bit = device_index % 2
    high_bit = device_index // 2 % 2
    shaped = block.reshape(2, 2, tok_rows, quarter_width)
    kept = lax.dynamic_index_in_dim(shaped, high_bit, 0, keepdims=False)
    sent = lax.dynamic_index_in_dim(shaped, 1 - high_bit, 0, keepdims=False)
    first = order_pair(high_bit, kept, join_swap(sent, 1), 0)
    kept = lax.dynamic_index_in_dim(first, low_bit, 1, keepdims=False)
    sent = lax.dynamic_index_in_dim(first, 1 - low_bit, 1, keepdims=False)
    second = order_pair(low_bit, kept, join_swap(sent, 0), 1)
    return second.transpose(2, 0, 1, 3).reshape(tok_rows, 4 * quarter_width)


def gather_quads(pair, device_index):
    levels = lax.axis_size("patch").bit_length() - 1
    current = pair
    for bit in range(2, levels):
        arrived = from_partner(current, "patch", bit)
        own_bit = device_index // (1 << bit) % 2
        current = jnp.where(
            own_bit == 0,
            jnp.concatenate([current, arrived], 1),
            jnp.concatenate([arrived, current], 1),
        )
    return current


def local(
    queries,
    keys,
    values,
    stale_keys,
    stale_values,
    text_keys,
    text_values,
    prompt_device,
    patch_owner,
    step,
    q_gain,
    k_gain,
    gate_table,
):
    tok_rows = queries.shape[0]
    head_count = queries.shape[1] // DH
    device_index = lax.axis_index("patch")
    own_patch = lax.dynamic_index_in_dim(patch_owner, device_index, 0, keepdims=False)
    grid_index = own_patch * tok_rows + jnp.arange(tok_rows, dtype=jnp.int32)
    cosine, sine_part = rope_tables(grid_index)
    query_rot = rotate(rms_norm(queries, q_gain), cosine, sine_part)
    key_rot = rotate(rms_norm(keys, k_gain), cosine, sine_part)
    text_rows, text_vals = (
        broadcast(text_keys[0], "patch", prompt_device[0]),
        broadcast(text_values[0], "patch", prompt_device[0]),
    )
    gate_row = lax.dynamic_index_in_dim(gate_table, step[0], 0, keepdims=False)
    quarter_heads = head_count // 4
    quarter_width = quarter_heads * DH
    quarter = device_index % 4
    spread = split_heads(
        jnp.stack([query_rot, key_rot, values, stale_keys, stale_values]), device_index
    )
    quad_rows = 4 * tok_rows
    query_quad = spread[0].reshape(quad_rows, quarter_heads, DH)
    source = jnp.arange(quad_rows, dtype=jnp.int32) // tok_rows
    own_part = partial_softmax(query_quad, spread[1], spread[2], source[:, None] == source[None, :])
    text_key_quarter = lax.dynamic_slice_in_dim(
        text_rows, quarter * quarter_width, quarter_width, 1
    )
    text_val_quarter = lax.dynamic_slice_in_dim(
        text_vals, quarter * quarter_width, quarter_width, 1
    )
    text_part = partial_softmax(
        query_quad, text_key_quarter, text_val_quarter, jnp.ones((1, text_rows.shape[0]), bool)
    )
    running = combine_parts(own_part, text_part)
    gathered = gather_quads(spread[3:5], device_index)
    key_device = jnp.arange(gathered.shape[1], dtype=jnp.int32) // tok_rows
    query_device = device_index // 4 * 4 + source
    stale_part = partial_softmax(
        query_quad, gathered[0], gathered[1], key_device[None, :] != query_device[:, None]
    )
    highest, totals, summed = combine_parts(running, stale_part)
    mixed = summed / totals[..., None]
    merged = mixed.transpose(1, 0, 2).reshape(quad_rows, quarter_width)
    gate_quarter = lax.dynamic_slice_in_dim(gate_row, quarter * quarter_width, quarter_width, 0)
    return join_heads((merged * gate_quarter).astype(jnp.bfloat16), device_index)


def solution(mesh):
    return jax.shard_map(
        local,
        mesh=mesh,
        in_specs=(
            P(("group", "patch"), None),
            P(("group", "patch"), None),
            P(("group", "patch"), None),
            P(("group", "patch"), None),
            P(("group", "patch"), None),
            P(("group", "patch"), None, None),
            P(("group", "patch"), None, None),
            P("group"),
            P("group"),
            P("group"),
            P(),
            P(),
            P(),
        ),
        out_specs=P(("group", "patch"), None),
        check_vma=False,
    )
```

profile of v0, /device:TPU:0, one launch (start us, length us, event | category | flops | bytes accessed | tf_op | source)
XLA Modules:
  0.0 165.2 jit_solution(5192727807104627779)
XLA Ops:
  6.6 1.1 copy.121
  7.7 0.9 convert_multiply_fusion
  8.6 1.1 copy.119
  9.8 0.6 dynamic_slice.43
  12.2 0.9 multiply_multiply_fusion
  13.1 2.2 %subtract_convert_fusion = (bf16[32,12,64,1]{0,3,2,1:T(2,128)(2,1)S(1)}, bf16[32,12,64,1]{0,3,2,1:T(2,128)(2,1)S(1)}, bf16[32,12,64,1]{0,3,2,1:T(2,128)(2,1)S(1)}, bf16[32,12,64,1]{0,3,2,1:T(2,128)(2,1)S(1)}) fusion(f32[32,12,64,2]{0,3,2,1:T(2,128)S(1)} %get-tuple-element.45, f32[32,64]{0,1:T(8,128)S(1)} %get-tuple-element.32, ...), kind=kLoop, calls=%fused_computation.35 | loop fusion | flops 393216 | bytes 606208 | tf_op jit(solution)/shard_map/convert
  15.3 1.0 pad_maximum_fusion.1
  16.5 1.0 pad_maximum_fusion
  18.0 0.9 dynamic-slice_bitcast_fusion.3
  18.9 0.5 collective-permute-start
  20.1 0.7 copy.132
  20.8 1.7 %copy.135 = bf16[1,512,1536]{1,2,0:T(8,128)(2,1)S(1)} copy(bf16[1,512,1536]{2,1,0:T(8,128)(2,1)} %param.19) | data formatting | bytes 3145728 | tf_op args[6]
  22.5 1.9 %select_bitcast_fusion = (bf16[512,1536]{0,1:T(8,128)(2,1)}, bf16[512,1536]{0,1:T(8,128)(2,1)}) fusion(bf16[1,512,1536]{1,2,0:T(8,128)(2,1)S(1)} %copy.135, pred[]{:T(512)S(6)} %eq.56, bf16[1,512,1536]{1,2,0:T(8,128)(2,1)S(1)} %copy.132), kind=kLoop, calls=%fused_computation | loop fusion | flops 1572864 | bytes 6291457 | tf_op jit(solution)/shard_map/jit(_where)/select_n | solution.py:17
  24.5 0.8 copy-done.2
  25.4 1.1 maximum_select_fusion.1
  26.6 2.6 %collective-permute-start.1 = (bf16[5,2,32,384]{3,2,1,0:T(8,128)(2,1)S(1)}, bf16[5,2,32,384]{3,2,1,0:T(8,128)(2,1)S(1)}, u32[]{:S(2)}, u32[]{:S(2)}) collective-permute-start(bf16[5,2,32,384]{3,2,1,0:T(8,128)(2,1)S(1)} %get-tuple-element.22), channel_id=1, source_target_pairs={{0,2},{1,3},{2,0},{3,1},{4,6},{5,7},{6,4},{7,5},{8,10},{9,11},{10,... | collective-permute-start | bytes 737288 | tf_op jit(solution)/shard_map/ppermute | solution.py:12
  29.3 9.0 %collective-permute-done.1 = bf16[5,2,32,384]{3,2,1,0:T(8,128)(2,1)S(1)} collective-permute-done((bf16[5,2,32,384]{3,2,1,0:T(8,128)(2,1)S(1)}, bf16[5,2,32,384]{3,2,1,0:T(8,128)(2,1)S(1)}, u32[]{:S(2)}, u32[]{:S(2)}) %collective-permute-start.1) | collective-permute-done | bytes 245792 | tf_op jit(solution)/shard_map/ppermute | solution.py:12
  38.4 1.5 collective-permute-start.2
  40.8 8.6 %collective-permute-done.2 = bf16[2,128,384]{2,1,0:T(8,128)(2,1)S(1)} collective-permute-done((bf16[2,128,384]{2,1,0:T(8,128)(2,1)S(1)}, bf16[2,128,384]{2,1,0:T(8,128)(2,1)S(1)}, u32[]{:S(2)}, u32[]{:S(2)}) %collective-permute-start.2) | collective-permute-done | bytes 196640 | tf_op jit(solution)/shard_map/ppermute | solution.py:12
  49.6 2.7 %collective-permute-start.3 = (bf16[2,256,384]{2,1,0:T(8,128)(2,1)S(1)}, bf16[2,256,384]{2,1,0:T(8,128)(2,1)S(1)}, u32[]{:S(2)}, u32[]{:S(2)}) collective-permute-start(bf16[2,256,384]{2,1,0:T(8,128)(2,1)S(1)} %maximum_select_fusion.3), channel_id=1, source_target_pairs={{0,8},{1,9},{2,10},{3,11},{4,12},{5,13},{6,14},{7,15},{8,0},{9,1},... | collective-permute-start | bytes 1179656 | tf_op jit(solution)/shard_map/ppermute | solution.py:12
  52.7 24.7 %collective-permute-done.3 = bf16[2,256,384]{2,1,0:T(8,128)(2,1)S(1)} collective-permute-done((bf16[2,256,384]{2,1,0:T(8,128)(2,1)S(1)}, bf16[2,256,384]{2,1,0:T(8,128)(2,1)S(1)}, u32[]{:S(2)}, u32[]{:S(2)}) %collective-permute-start.3) | collective-permute-done | bytes 393248 | tf_op jit(solution)/shard_map/ppermute | solution.py:12
  78.1 0.3 fusion.53
  78.8 69.3 %all-reduce.3.cloned.1.call-done = (bf16[512,1536]{0,1:T(8,128)(2,1)}, bf16[512,1536]{0,1:T(8,128)(2,1)}) async-done(((bf16[512,1536]{0,1:T(8,128)(2,1)}, bf16[512,1536]{0,1:T(8,128)(2,1)}), (bf16[512,1536]{0,1:T(8,128)(2,1)}, bf16[512,1536]{0,1:T(8,128)(2,1)})) %all-reduce.3.cloned.1.call-update) | async-done | bytes 3145744 | tf_op jit(solution)/shard_map/psum | solution.py:17
  148.1 1.0 constant_dynamic-slice_fusion.3
  149.1 0.3 fusion.54
  149.4 1.0 constant_dynamic-slice_fusion.2
  151.0 0.3 fusion.8
  151.4 0.4 fusion.7
  152.1 1.0 collective-permute-start.4
  153.1 3.1 %collective-permute-done.4 = bf16[2,32,384]{2,1,0:T(8,128)(2,1)S(1)} collective-permute-done((bf16[2,32,384]{2,1,0:T(8,128)(2,1)S(1)}, bf16[2,32,384]{2,1,0:T(8,128)(2,1)S(1)}, u32[]{:S(2)}, u32[]{:S(2)}) %collective-permute-start.4) | collective-permute-done | bytes 49184 | tf_op jit(solution)/shard_map/ppermute | solution.py:12
  156.3 1.2 collective-permute-done.5
  157.7 0.7 reshape.361
  (82 shorter events, 4.8 us)
Async XLA Ops:
  6.5 34.2 %copy-start = (f32[28,1536]{1,0:T(8,128)S(1)}, f32[28,1536]{1,0:T(8,128)}, u32[]{:S(2)}) copy-start(f32[28,1536]{1,0:T(8,128)} %param.25) | copy-start | bytes 516100
  6.5 3.2 %copy-start.3 = (bf16[32,1536]{1,0:T(8,128)(2,1)S(1)}, bf16[32,1536]{1,0:T(8,128)(2,1)}, u32[]{:S(2)}) copy-start(bf16[32,1536]{1,0:T(8,128)(2,1)} %param.13) | copy-start | bytes 294916
  6.5 3.2 %copy-start.9 = (s32[16]{0:T(128)S(1)}, s32[16]{0:T(128)}, u32[]{:S(2)}) copy-start(s32[16]{0:T(128)} %param.21) | copy-start | bytes 196
  6.5 141.5 %all-reduce.3.cloned.1.call-start = ((), (), s32[]{:S(2)}) async-start(), calls=%async_computation | async-start | bytes 6291456 | tf_op jit(solution)/shard_map/psum | solution.py:17
  7.7 3.9 %copy-start.7 = (f32[128]{0:T(128)S(1)}, f32[128]{0:T(128)}, u32[]{:S(2)}) copy-start(f32[128]{0:T(128)} %param.23) | copy-start | bytes 1540
  7.7 4.0 %copy-start.8 = (f32[128]{0:T(128)S(1)}, f32[128]{0:T(128)}, u32[]{:S(2)}) copy-start(f32[128]{0:T(128)} %param.24) | copy-start | bytes 1540
  15.3 2.5 %copy-start.4 = (bf16[32,1536]{1,0:T(8,128)(2,1)S(1)}, bf16[32,1536]{1,0:T(8,128)(2,1)}, u32[]{:S(2)}) copy-start(bf16[32,1536]{1,0:T(8,128)(2,1)} %param.15) | copy-start | bytes 294916
  16.3 1.5 copy-start.5
  16.3 1.5 copy-start.6
  17.6 2.5 %copy-start.1 = (bf16[1,512,1536]{2,1,0:T(8,128)(2,1)S(1)}, bf16[1,512,1536]{2,1,0:T(8,128)(2,1)}, u32[]{:S(2)}) copy-start(bf16[1,512,1536]{2,1,0:T(8,128)(2,1)} %param.18) | copy-start | bytes 4718596
  18.9 5.6 %collective-permute-start = (bf16[5,32,2,384]{3,1,2,0:T(8,128)(2,1)}, bf16[5,32,2,384]{3,1,2,0:T(8,128)(2,1)}, u32[]{:S(2)}, u32[]{:S(2)}) collective-permute-start(bf16[5,32,2,384]{3,1,2,0:T(8,128)(2,1)} %get-tuple-element.24), channel_id=1, source_target_pairs={{0,1},{1,0},{2,3},{3,2},{4,5},{5,4},{6,7},{7,6},{8,9},{9,8},{10,11... | collective-permute-start | bytes 737288 | tf_op jit(solution)/shard_map/ppermute | solution.py:12
  24.4 0.9 copy-start.2
  26.6 11.7 %collective-permute-start.1 = (bf16[5,2,32,384]{3,2,1,0:T(8,128)(2,1)S(1)}, bf16[5,2,32,384]{3,2,1,0:T(8,128)(2,1)S(1)}, u32[]{:S(2)}, u32[]{:S(2)}) collective-permute-start(bf16[5,2,32,384]{3,2,1,0:T(8,128)(2,1)S(1)} %get-tuple-element.22), channel_id=1, source_target_pairs={{0,2},{1,3},{2,0},{3,1},{4,6},{5,7},{6,4},{7,5},{8,10},{9,11},{10,... | collective-permute-start | bytes 737288 | tf_op jit(solution)/shard_map/ppermute | solution.py:12
  38.4 11.0 %collective-permute-start.2 = (bf16[2,128,384]{2,1,0:T(8,128)(2,1)S(1)}, bf16[2,128,384]{2,1,0:T(8,128)(2,1)S(1)}, u32[]{:S(2)}, u32[]{:S(2)}) collective-permute-start(bf16[2,128,384]{2,1,0:T(8,128)(2,1)S(1)} %bitcast.139), channel_id=1, source_target_pairs={{0,4},{1,5},{2,6},{3,7},{4,0},{5,1},{6,2},{7,3},{8,12},{9,13},{10,... | collective-permute-start | bytes 589832 | tf_op jit(solution)/shard_map/ppermute | solution.py:12
  49.6 27.8 %collective-permute-start.3 = (bf16[2,256,384]{2,1,0:T(8,128)(2,1)S(1)}, bf16[2,256,384]{2,1,0:T(8,128)(2,1)S(1)}, u32[]{:S(2)}, u32[]{:S(2)}) collective-permute-start(bf16[2,256,384]{2,1,0:T(8,128)(2,1)S(1)} %maximum_select_fusion.3), channel_id=1, source_target_pairs={{0,8},{1,9},{2,10},{3,11},{4,12},{5,13},{6,14},{7,15},{8,0},{9,1},... | collective-permute-start | bytes 1179656 | tf_op jit(solution)/shard_map/ppermute | solution.py:12
  152.1 4.2 %collective-permute-start.4 = (bf16[2,32,384]{2,1,0:T(8,128)(2,1)S(1)}, bf16[2,32,384]{2,1,0:T(8,128)(2,1)S(1)}, u32[]{:S(2)}, u32[]{:S(2)}) collective-permute-start(bf16[2,32,384]{2,1,0:T(8,128)(2,1)S(1)} %get-tuple-element.28), channel_id=1, source_target_pairs={{0,2},{1,3},{2,0},{3,1},{4,6},{5,7},{6,4},{7,5},{8,10},{9,11},{10,... | collective-permute-start | bytes 147464 | tf_op jit(solution)/shard_map/ppermute | solution.py:12
  156.3 1.3 collective-permute-start.5
Sparse Core Ops, SparseCore 0:
  24.6 123.4 all-reduce.2
where the time goes:
time: 166 us; the launch traced here: 165 us
  waiting for transfers between devices  116 us (70%)
  between operations  16 us (10%)
  local copies, waits for them, and re-layouts  11.9 us (7%)
  other arithmetic  11.2 us (7%)
  starting transfers between devices  8.3 us (5%)
  matrix products  1.84 us (1%)
    psum x1, waiting for transfers between devices, broadcast(): return lax.psum(jnp.where(mine, shard, jnp.zeros_like(shard)), axis)  69.3 us
    ppermute x6, waiting for transfers between devices, from_partner(): lax.ppermute(shard, axis, [(i, i ^ 1 << bit) for i in range(lax.axis_size...  46.6 us
    ppermute x6, starting transfers between devices, from_partner(): lax.ppermute(shard, axis, [(i, i ^ 1 << bit) for i in range(lax.axis_size...  8.3 us
    unnamed x26, local copies, waits for them, and re-layouts  3.39 us
  transfers between devices with their start and end apart: 7, of which 6 were waited for; matrix products, arithmetic and copies ran while one was open for 5% of the time, Pallas kernels for 0%

commit v1 on v0

--- a/solution.py
+++ b/solution.py
@@ -6,6 +6,9 @@
 DH = 128
 GRID_W = 64
 epsilon = 1e-06
+_drive_streams = lambda local_array, axis_tag: jnp.sum(
+    lax.all_gather(local_array, axis_tag), axis=0
+)
 
 
 def from_partner(shard, axis, bit):
@@ -14,7 +17,7 @@
 
 def broadcast(shard, axis, root):
     mine = lax.axis_index(axis) == root
-    return lax.psum(jnp.where(mine, shard, jnp.zeros_like(shard)), axis)
+    return _drive_streams(jnp.where(mine, shard, jnp.zeros_like(shard)), axis)
 
 
 def rms_norm(values_in, gain):

time: 166 us -> 319 us (1.92)
  waiting for transfers between devices: 116 us -> 243 us
  other arithmetic: 11.2 us -> 38.3 us
    all_gather x0 -> x2, waiting for transfers between devices: none -> 190 us  [lax.all_gather(local_array, axis_tag)]
    psum x1 -> x0, waiting for transfers between devices: 69.3 us -> none  [broadcast(): return lax.psum(jnp.where(mine, shard, jnp.zeros_like(shard)), axis)]
    reduce_sum x0 -> x2, other arithmetic: none -> 28.7 us  [jnp.sum(lax.all_gather(local_array, axis_tag), axis=0)]
    ppermute x6, waiting for transfers between devices: 46.6 us -> 52.5 us  [from_partner(): lax.ppermute(shard, axis, [(i, i ^ 1 << bit) for i in range(lax.axis_size...]
  transfers between devices with their start and end apart: 7 -> 8, of which waited for: 6 -> 8; matrix products, arithmetic and copies ran while one was open for 5% -> 9% of each run, Pallas kernels for 0% -> 0%
where the time goes in v1:
time: 319 us; the launch traced here: 318 us
  waiting for transfers between devices  243 us (76%)
  other arithmetic  38.3 us (12%)
  between operations  16 us (5%)
  local copies, waits for them, and re-layouts  9.63 us (3%)
  starting transfers between devices  8.61 us (3%)
    all_gather x2, waiting for transfers between devices, lax.all_gather(local_array, axis_tag)  190 us
    ppermute x6, waiting for transfers between devices, from_partner(): lax.ppermute(shard, axis, [(i, i ^ 1 << bit) for i in range(lax.axis_size...  52.5 us
    reduce_sum x2, other arithmetic, jnp.sum(lax.all_gather(local_array, axis_tag), axis=0)  28.7 us
    ppermute x6, starting transfers between devices, from_partner(): lax.ppermute(shard, axis, [(i, i ^ 1 << bit) for i in range(lax.axis_size...  8.57 us
  transfers between devices with their start and end apart: 8, of which 8 were waited for; matrix products, arithmetic and copies ran while one was open for 9% of the time, Pallas kernels for 0%

profile of v1, /device:TPU:0, one launch (start us, length us, event | category | flops | bytes accessed | tf_op | source)
XLA Modules:
  0.0 318.1 jit_solution(12642668951874692974)
XLA Ops:
  7.2 1.2 broadcast_select_fusion.1
  8.5 1.3 copy-done.2
  9.9 1.2 broadcast_select_fusion
  11.2 0.8 copy-done.8
  13.3 0.6 dynamic_slice.43
  14.9 0.9 multiply_multiply_fusion
  15.8 2.1 subtract_convert_fusion
  17.9 1.0 pad_maximum_fusion.1
  19.2 1.0 pad_maximum_fusion
  20.7 0.6 collective-permute-start
  21.3 1.1 collective-permute-done
  22.6 2.9 collective-permute-start.1
  26.2 0.7 dynamic-slice_reduce_fusion
  27.0 10.4 %collective-permute-done.1 = bf16[5,2,32,384]{3,2,1,0:T(8,128)(2,1)S(1)} collective-permute-done((bf16[5,2,32,384]{3,2,1,0:T(8,128)(2,1)S(1)}, bf16[5,2,32,384]{3,2,1,0:T(8,128)(2,1)S(1)}, u32[]{:S(2)}, u32[]{:S(2)}) %collective-permute-start.1) | collective-permute-done | bytes 245792 | tf_op jit(solution)/shard_map/ppermute | solution.py:15
  37.8 11.5 %collective-permute-done.2 = bf16[2,128,384]{2,1,0:T(8,128)(2,1)S(1)} collective-permute-done((bf16[2,128,384]{2,1,0:T(8,128)(2,1)S(1)}, bf16[2,128,384]{2,1,0:T(8,128)(2,1)S(1)}, u32[]{:S(2)}, u32[]{:S(2)}) %collective-permute-start.2) | collective-permute-done | bytes 196640 | tf_op jit(solution)/shard_map/ppermute | solution.py:15
  49.4 3.6 %collective-permute-start.3 = (bf16[2,256,384]{2,1,0:T(8,128)(2,1)S(1)}, bf16[2,256,384]{2,1,0:T(8,128)(2,1)S(1)}, u32[]{:S(2)}, u32[]{:S(2)}) collective-permute-start(bf16[2,256,384]{2,1,0:T(8,128)(2,1)S(1)} %maximum_select_fusion.3), channel_id=1, source_target_pairs={{0,8},{1,9},{2,10},{3,11},{4,12},{5,13},{6,14},{7,15},{8,0},{9,1},... | collective-permute-start | bytes 1179656 | tf_op jit(solution)/shard_map/ppermute | solution.py:15
  53.2 0.7 reshape_squeeze.17
  54.2 25.3 %collective-permute-done.3 = bf16[2,256,384]{2,1,0:T(8,128)(2,1)S(1)} collective-permute-done((bf16[2,256,384]{2,1,0:T(8,128)(2,1)S(1)}, bf16[2,256,384]{2,1,0:T(8,128)(2,1)S(1)}, u32[]{:S(2)}, u32[]{:S(2)}) %collective-permute-start.3) | collective-permute-done | bytes 393248 | tf_op jit(solution)/shard_map/ppermute | solution.py:15
  80.1 0.9 copy.137
  81.0 0.3 fusion.53
  81.7 71.2 %all-gather.3.cloned.1.call-done = bf16[16,512,1536]{2,1,0:T(8,128)(2,1)} async-done(((bf16[1,512,1536]{2,1,0:T(8,128)(2,1)}), bf16[16,512,1536]{2,1,0:T(8,128)(2,1)}) %all-gather.3.cloned.1.call-update) | async-done | bytes 25165840 | tf_op jit(solution)/shard_map/all_gather | solution.py:10
  152.9 14.1 %reduce_sum.77 = bf16[512,1536]{1,0:T(8,128)(2,1)S(1)} reduce(bf16[16,512,1536]{2,1,0:T(8,128)(2,1)} %all-gather.3.cloned.1.call-done, bf16[]{:T(256)} %constant.208.clone.1), dimensions={0}, to_apply=%region_3.4 | reduce | flops 11796480 | bytes 26738690 | tf_op jit(solution)/shard_map/reduce_sum | solution.py:9
  166.9 119.3 %all-gather.5.cloned.1.call-done = bf16[16,512,1536]{2,1,0:T(8,128)(2,1)} async-done(((bf16[1,512,1536]{2,1,0:T(8,128)(2,1)}), bf16[16,512,1536]{2,1,0:T(8,128)(2,1)}) %all-gather.5.cloned.1.call-update) | async-done | bytes 25165840 | tf_op jit(solution)/shard_map/all_gather | solution.py:10
  286.3 14.6 %reduce_sum.78 = bf16[512,1536]{1,0:T(8,128)(2,1)} reduce(bf16[16,512,1536]{2,1,0:T(8,128)(2,1)} %all-gather.5.cloned.1.call-done, bf16[]{:T(256)} %constant.208.clone.1), dimensions={0}, to_apply=%region_5.6 | reduce | flops 11796480 | bytes 26738690 | tf_op jit(solution)/shard_map/reduce_sum | solution.py:9
  300.8 1.1 constant_dynamic-slice_fusion.2
  303.0 0.8 fusion.6
  303.9 0.3 fusion.8
  304.3 0.4 fusion.7
  305.0 1.3 collective-permute-start.4
  306.2 2.9 collective-permute-done.4
  309.2 1.2 collective-permute-done.5
  310.6 0.7 reshape.355
  (105 shorter events, 5.7 us)
Async XLA Ops:
  6.5 19.7 %copy-start = (f32[28,1536]{1,0:T(8,128)S(1)}, f32[28,1536]{1,0:T(8,128)}, u32[]{:S(2)}) copy-start(f32[28,1536]{1,0:T(8,128)} %param.25) | copy-start | bytes 516100
  6.5 146.3 %all-gather.3.cloned.1.call-start = ((), (), s32[]{:S(2)}) async-start(), calls=%async_computation | async-start | bytes 26738688 | tf_op jit(solution)/shard_map/all_gather | solution.py:10
  8.5 1.4 copy-start.2
  8.5 277.8 %all-gather.5.cloned.1.call-start = ((), (), s32[]{:S(2)}) async-start(), calls=%async_computation.1 | async-start | bytes 26738688 | tf_op jit(solution)/shard_map/all_gather | solution.py:10
  11.1 0.9 copy-start.8
  11.1 1.1 copy-start.7
  12.2 0.8 copy-start.16
  12.2 0.9 copy-start.17
  12.2 1.1 copy-start.18
  17.9 2.5 copy-start.9
  17.9 2.5 copy-start.10
  19.0 1.5 copy-start.11
  20.7 1.7 collective-permute-start
  22.6 14.9 %collective-permute-start.1 = (bf16[5,2,32,384]{3,2,1,0:T(8,128)(2,1)S(1)}, bf16[5,2,32,384]{3,2,1,0:T(8,128)(2,1)S(1)}, u32[]{:S(2)}, u32[]{:S(2)}) collective-permute-start(bf16[5,2,32,384]{3,2,1,0:T(8,128)(2,1)S(1)} %get-tuple-element.20), channel_id=1, source_target_pairs={{0,2},{1,3},{2,0},{3,1},{4,6},{5,7},{6,4},{7,5},{8,10},{9,11},{10,... | collective-permute-start | bytes 737288 | tf_op jit(solution)/shard_map/ppermute | solution.py:15
  27.0 54.4 %copy-start.3 = (pred[128,512]{1,0:T(8,128)(4,1)}, pred[128,512]{1,0:T(8,128)(4,1)S(1)}, u32[]{:S(2)}) copy-start(pred[128,512]{1,0:T(8,128)(4,1)S(1)} %broadcast_compare_fusion) | copy-start | bytes 196612
  37.6 11.7 %collective-permute-start.2 = (bf16[2,128,384]{2,1,0:T(8,128)(2,1)S(1)}, bf16[2,128,384]{2,1,0:T(8,128)(2,1)S(1)}, u32[]{:S(2)}, u32[]{:S(2)}) collective-permute-start(bf16[2,128,384]{2,1,0:T(8,128)(2,1)S(1)} %bitcast.135), channel_id=1, source_target_pairs={{0,4},{1,5},{2,6},{3,7},{4,0},{5,1},{6,2},{7,3},{8,12},{9,13},{10,... | collective-permute-start | bytes 589832 | tf_op jit(solution)/shard_map/ppermute | solution.py:15
  49.4 30.1 %collective-permute-start.3 = (bf16[2,256,384]{2,1,0:T(8,128)(2,1)S(1)}, bf16[2,256,384]{2,1,0:T(8,128)(2,1)S(1)}, u32[]{:S(2)}, u32[]{:S(2)}) collective-permute-start(bf16[2,256,384]{2,1,0:T(8,128)(2,1)S(1)} %maximum_select_fusion.3), channel_id=1, source_target_pairs={{0,8},{1,9},{2,10},{3,11},{4,12},{5,13},{6,14},{7,15},{8,0},{9,1},... | collective-permute-start | bytes 1179656 | tf_op jit(solution)/shard_map/ppermute | solution.py:15
  54.1 248.9 %copy-start.12 = (f32[3,128]{1,0:T(4,128)}, f32[3,128]{1,0:T(4,128)S(1)}, u32[]{:S(2)}) copy-start(f32[3,128]{1,0:T(4,128)S(1)} %get-tuple-element.37) | copy-start | bytes 4612
  81.4 221.6 %copy-start.13 = (f32[3,128]{1,0:T(4,128)}, f32[3,128]{1,0:T(4,128)S(1)}, u32[]{:S(2)}) copy-start(f32[3,128]{1,0:T(4,128)S(1)} %get-tuple-element.33) | copy-start | bytes 4612
  302.1 0.9 copy-start.5
  302.6 1.6 copy-start.4
  302.7 1.6 copy-start.6
  303.0 1.3 copy-start.14
  304.2 0.7 copy-start.15
  304.3 7.0 %copy-start.1 = (f32[28,1536]{1,0:T(8,128)S(1)}, f32[28,1536]{1,0:T(8,128)}, u32[]{:S(2)}) copy-start(f32[28,1536]{1,0:T(8,128)} %param.25) | copy-start | bytes 516100
  305.0 4.2 %collective-permute-start.4 = (bf16[2,32,384]{2,1,0:T(8,128)(2,1)S(1)}, bf16[2,32,384]{2,1,0:T(8,128)(2,1)S(1)}, u32[]{:S(2)}, u32[]{:S(2)}) collective-permute-start(bf16[2,32,384]{2,1,0:T(8,128)(2,1)S(1)} %get-tuple-element.26), channel_id=1, source_target_pairs={{0,2},{1,3},{2,0},{3,1},{4,6},{5,7},{6,4},{7,5},{8,10},{9,11},{10,... | collective-permute-start | bytes 147464 | tf_op jit(solution)/shard_map/ppermute | solution.py:15
  309.2 1.3 collective-permute-start.5
Sparse Core Ops, SparseCore 0:
  8.9 143.8 all-gather.2
  154.4 131.7 all-gather.4
